TPU v7x, 32 devices: a whole 2x2x4 slice. The times are simulated.
32 devices in a mesh: gx: 4 (over z), gy: 4 (over y, x), gz: 2 (over core).
Axes of the slice: x: 2, y: 2, z: 4, core: 2. Of those that a mesh axis runs over, the one named last changes fastest.
Arguments:
- velocity: float32 [3, 64, 64, 256], P(None, 'gx', 'gy', 'gz'), may hold values from -6 to 6
Outputs:
- stress_residual: float32 [6, 2048], P(None, ('gx', 'gy', 'gz'))
- coefficients: float32 [96, 6], replicated
All inputs are finite; a program needn't handle non-finite values.
Results may differ from a plain program's by a relative error of at most 0.0042.
Values may be sent and summed in bfloat16 or wider, within the bound.
No kernel may reach another device: no remote copies, remote signals or barrier semaphores. Data moves between devices by JAX's collectives and lax.ppermute only.
A program may use at most 64 MiB of HBM per device.

v0:
```python
import jax
import jax.numpy as jnp
import numpy as np
from jax import lax
from jax.sharding import PartitionSpec as P

PRECISE = lax.Precision.HIGHEST
INDEX_PAIRS = ((0, 0), (1, 1), (2, 2), (0, 1), (0, 2), (1, 2))
WIDTHS = (3.0, 6.0, 12.0)


def extended(block, sides, width):
    for axis, dim in sides:
        count = lax.axis_size(axis)
        forward = [(i, i + 1) for i in range(count - 1)]
        forward.append((count - 1, 0))
        backward = [(target, source) for source, target in forward]
        low = lax.ppermute(
            lax.slice_in_dim(block, block.shape[dim] - width, None, axis=dim), axis, forward
        )
        high = lax.ppermute(lax.slice_in_dim(block, 0, width, axis=dim), axis, backward)
        block = jnp.concatenate([low, block, high], axis=dim)
    return block


def window_table(combos):
    weights_table = np.zeros((len(combos), 16), np.float32)
    for row_index in range(len(combos)):
        box_width, offset = combos[row_index]
        low_edge = 7.5 + offset - box_width / 2.0
        high_edge = 7.5 + offset + box_width / 2.0
        for cell_index in range(16):
            cell_share = min(cell_index + 0.5, high_edge) - max(cell_index - 0.5, low_edge)
            weights_table[row_index, cell_index] = max(cell_share, 0.0) / box_width
    return weights_table


def velocity_combos():
    return [(box_width, offset) for box_width in WIDTHS for offset in (-2.0, 0.0, 2.0)]


def product_combos():
    return [(3.0, 0.0), (12.0, 0.0)]


def matrix_product(left_matrix, right_matrix):
    return [
        [
            left_matrix[i][0] * right_matrix[0][j]
            + left_matrix[i][1] * right_matrix[1][j]
            + left_matrix[i][2] * right_matrix[2][j]
            for j in range(3)
        ]
        for i in range(3)
    ]


def pick_pairs(matrix):
    return [matrix[i][j] for i, j in INDEX_PAIRS]


def build_rows(box_means, pair_means):
    feature_rows = []
    centre_values = []
    for width_index in range(3):
        middle = 3 * width_index + 1
        scaled = WIDTHS[width_index] ** 2 * 0.25

        def offset_value(component, direction, step_size):
            position_list = [middle, middle, middle]
            position_list[direction] = middle + step_size
            return box_means[component, position_list[0], position_list[1], position_list[2]]

        centre_values.append([box_means[i, middle, middle, middle] for i in range(3)])
        gradient = [
            [(offset_value(i, j, 1) - offset_value(i, j, -1)) * scaled for j in range(3)]
            for i in range(3)
        ]
        strain = [[(gradient[i][j] + gradient[j][i]) * 0.5 for j in range(3)] for i in range(3)]
        spin_part = [[(gradient[i][j] - gradient[j][i]) * 0.5 for j in range(3)] for i in range(3)]
        square_strain = matrix_product(strain, strain)
        first_order = matrix_product(strain, spin_part)
        second_order = matrix_product(spin_part, strain)
        commutator = [[first_order[i][j] - second_order[i][j] for j in range(3)] for i in range(3)]
        spin_square = matrix_product(spin_part, spin_part)
        magnitude = sum((strain[i][j] * strain[i][j] for i in range(3) for j in range(3)))
        feature_rows += (
            pick_pairs(strain)
            + pick_pairs(square_strain)
            + pick_pairs(commutator)
            + pick_pairs(spin_square)
        )
        feature_rows += [magnitude * entry for entry in pick_pairs(strain)]
    small_box = centre_values[0]
    large_box = centre_values[2]
    feature_rows += [
        pair_means[index, 0] - small_box[i] * small_box[j]
        for index, (i, j) in enumerate(INDEX_PAIRS)
    ]
    target_rows = [
        pair_means[index, 1] - large_box[i] * large_box[j]
        for index, (i, j) in enumerate(INDEX_PAIRS)
    ]
    return (jnp.stack(feature_rows), jnp.stack(target_rows))


def solve_fit(gram_matrix, sample_total):
    scales = jnp.sqrt(jnp.diagonal(gram_matrix) / sample_total + 1e-06)
    feature_scale = scales[:96]
    normal = gram_matrix[:96, :96] / (
        sample_total * feature_scale[:, None] * feature_scale[None, :]
    ) + 0.1 * jnp.eye(96, dtype=jnp.float32)
    target_side = gram_matrix[:96, 96:] / (sample_total * feature_scale[:, None])
    factor = jnp.linalg.cholesky(normal)
    solved = jax.scipy.linalg.cho_solve((factor, True), target_side)
    return (solved / feature_scale[:, None], scales[96:])


def axis_weights(length, weights_table):
    sample_count = length // 8
    combo_count = weights_table.shape[0]
    full_table = np.zeros((sample_count * combo_count, length + 8), np.float32)
    for sample_index in range(sample_count):
        full_table[
            sample_index * combo_count : (sample_index + 1) * combo_count,
            8 * sample_index : 8 * sample_index + 16,
        ] = weights_table
    return jnp.asarray(full_table)


def windowed(wide_field, weights_table):
    along_z = jnp.einsum(
        "cxyz,kz->cxyk",
        wide_field,
        axis_weights(wide_field.shape[3] - 8, weights_table),
        precision=PRECISE,
    )
    along_y = jnp.einsum(
        "cxyk,jy->cxjk",
        along_z,
        axis_weights(wide_field.shape[2] - 8, weights_table),
        precision=PRECISE,
    )
    return jnp.einsum(
        "cxjk,ix->cijk",
        along_y,
        axis_weights(wide_field.shape[1] - 8, weights_table),
        precision=PRECISE,
    )


def shards(velocity):
    rounded = velocity.astype(jnp.bfloat16)
    padded = extended(rounded, (("gx", 1), ("gy", 2), ("gz", 3)), 4)
    wide_field = padded.astype(jnp.float32)
    count_x = velocity.shape[1] // 8
    count_y = velocity.shape[2] // 8
    count_z = velocity.shape[3] // 8
    samples = count_x * count_y * count_z
    box_means = windowed(wide_field, window_table(velocity_combos()))
    box_means = box_means.reshape(3, count_x, 9, count_y, 9, count_z, 9)
    box_means = jnp.transpose(box_means, (0, 2, 4, 6, 1, 3, 5)).reshape(3, 9, 9, 9, samples)
    pair_field = jnp.stack([wide_field[i] * wide_field[j] for i, j in INDEX_PAIRS])
    pair_means = windowed(pair_field, window_table(product_combos())).reshape(
        6, count_x, 2, count_y, 2, count_z, 2
    )
    pair_means = jnp.stack(
        [pair_means[:, :, 0, :, 0, :, 0], pair_means[:, :, 1, :, 1, :, 1]], axis=1
    )
    pair_means = pair_means.reshape(6, 2, samples)
    features, targets = build_rows(box_means, pair_means)
    stacked = jnp.concatenate([features, targets], axis=0)
    local_gram = jnp.dot(stacked, stacked.T, precision=PRECISE, preferred_element_type=jnp.float32)
    gram_matrix = lax.psum(local_gram, ("gx", "gy", "gz"))
    sample_total = float(samples * lax.axis_size("gx") * lax.axis_size("gy") * lax.axis_size("gz"))
    coefficients, target_scale = solve_fit(gram_matrix, sample_total)
    predicted = jnp.dot(
        coefficients.T, features, precision=PRECISE, preferred_element_type=jnp.float32
    )
    residual = (targets - predicted) / target_scale[:, None]
    return (residual, coefficients)


def solution(mesh):
    in_specs = (P(None, "gx", "gy", "gz"),)
    out_specs = (P(None, ("gx", "gy", "gz")), P())
    return jax.shard_map(shards, mesh=mesh, in_specs=in_specs, out_specs=out_specs, check_vma=False)
```

profile of v0, /device:TPU:0, one launch (start us, length us, event | category | flops | bytes accessed | tf_op | source)
XLA Modules:
  0.0 118.4 jit_solution(10109509089073360371)
XLA Ops:
  0.6 1.0 convert_element_type.7
  1.7 3.1 %collective-permute-start = (bf16[3,4,16,128]{3,2,1,0:T(8,128)(2,1)S(1)}, bf16[3,4,16,128]{3,2,1,0:T(8,128)(2,1)S(1)}, u32[]{:S(2)}, u32[]{:S(2)}) collective-permute-start(bf16[3,4,16,128]{3,2,1,0:T(8,128)(2,1)S(1)} %get-tuple-element.102), channel_id=1, source_target_pairs={{0,8},{8,16},{16,24},{24,0},{1,9},{9,17},{17,25},{25,1},{2,10},{10... | collective-permute-start | bytes 147464 | tf_op jit(solution)/shard_map/ppermute | solution.py:18
  4.8 2.1 %collective-permute-start.1 = (bf16[3,4,16,128]{3,2,1,0:T(8,128)(2,1)S(1)}, bf16[3,4,16,128]{3,2,1,0:T(8,128)(2,1)S(1)}, u32[]{:S(2)}, u32[]{:S(2)}) collective-permute-start(bf16[3,4,16,128]{3,2,1,0:T(8,128)(2,1)S(1)} %get-tuple-element.103), channel_id=1, source_target_pairs={{8,0},{16,8},{24,16},{0,24},{9,1},{17,9},{25,17},{1,25},{10,2},{18... | collective-permute-start | bytes 147464 | tf_op jit(solution)/shard_map/ppermute | solution.py:21
  6.9 2.1 %collective-permute-done = bf16[3,4,16,128]{3,2,1,0:T(8,128)(2,1)S(1)} collective-permute-done((bf16[3,4,16,128]{3,2,1,0:T(8,128)(2,1)S(1)}, bf16[3,4,16,128]{3,2,1,0:T(8,128)(2,1)S(1)}, u32[]{:S(2)}, u32[]{:S(2)}) %collective-permute-start) | collective-permute-done | bytes 49184 | tf_op jit(solution)/shard_map/ppermute | solution.py:18
  9.0 0.4 collective-permute-done.1
  9.5 1.5 %collective-permute-start.2 = (bf16[3,24,4,128]{3,2,1,0:T(4,128)(2,1)S(1)}, bf16[3,24,4,128]{3,2,1,0:T(4,128)(2,1)S(1)}, u32[]{:S(2)}, u32[]{:S(2)}) collective-permute-start(bf16[3,24,4,128]{3,2,1,0:T(4,128)(2,1)S(1)} %get-tuple-element.100), channel_id=1, source_target_pairs={{0,2},{2,4},{4,6},{6,0},{1,3},{3,5},{5,7},{7,1},{8,10},{10,12},{12... | collective-permute-start | bytes 221192 | tf_op jit(solution)/shard_map/ppermute | solution.py:18
  11.0 1.4 %collective-permute-start.3 = (bf16[3,24,4,128]{3,2,1,0:T(4,128)(2,1)S(1)}, bf16[3,24,4,128]{3,2,1,0:T(4,128)(2,1)S(1)}, u32[]{:S(2)}, u32[]{:S(2)}) collective-permute-start(bf16[3,24,4,128]{3,2,1,0:T(4,128)(2,1)S(1)} %get-tuple-element.101), channel_id=1, source_target_pairs={{2,0},{4,2},{6,4},{0,6},{3,1},{5,3},{7,5},{1,7},{10,8},{12,10},{14... | collective-permute-start | bytes 221192 | tf_op jit(solution)/shard_map/ppermute | solution.py:21
  12.5 2.3 %collective-permute-done.2 = bf16[3,24,4,128]{3,2,1,0:T(4,128)(2,1)S(1)} collective-permute-done((bf16[3,24,4,128]{3,2,1,0:T(4,128)(2,1)S(1)}, bf16[3,24,4,128]{3,2,1,0:T(4,128)(2,1)S(1)}, u32[]{:S(2)}, u32[]{:S(2)}) %collective-permute-start.2) | collective-permute-done | bytes 73760 | tf_op jit(solution)/shard_map/ppermute | solution.py:18
  14.8 0.8 collective-permute-done.3
  15.6 0.2 pad_maximum_fusion.1
  15.9 0.2 fusion.156
  16.2 0.5 collective-permute-start.5
  16.7 1.3 %collective-permute-done.4 = bf16[3,24,24,4]{3,2,1,0:T(8,128)(2,1)S(1)} collective-permute-done((bf16[3,24,24,4]{3,2,1,0:T(8,128)(2,1)S(1)}, bf16[3,24,24,4]{3,2,1,0:T(8,128)(2,1)S(1)}, u32[]{:S(2)}, u32[]{:S(2)}) %collective-permute-start.4) | collective-permute-done | bytes 13856 | tf_op jit(solution)/shard_map/ppermute | solution.py:18
  17.9 0.6 collective-permute-done.5
  18.6 1.3 %fusion.124 = f32[3,24,24,144]{3,2,1,0:T(8,128)S(1)} fusion(f32[144,136,1,1]{0,1,3,2:T(8,128)S(1)} %copy-done.8, bf16[3,24,24,4]{3,2,1,0:T(8,128)(2,1)S(1)} %collective-permute-done.5, bf16[3,24,4,128]{3,2,1,0:T(4,128)(2,1)S(1)} %collective-permute-done.3, bf16[3,4,16,128]{3,2,1,0:T(8,128)(2,1)S(1)} %collective-permute-done.1, ...), kind=kOutput, calls=%fused_computation.402 | convolution fusion | flops 409383936 | bytes 1543680 | tf_op jit(solution)/shard_map/cxyz,kz->cxyk/dot_general | solution.py:132
  19.9 1.6 %convolution_bitcast_fusion = f32[3,24,18,144]{3,2,1,0:T(8,128)S(1)} fusion(f32[3,24,24,144]{3,2,1,0:T(8,128)S(1)} %fusion.124, f32[18,24,1,1]{1,0,3,2:T(8,128)S(1)} %copy-done.4), kind=kOutput, calls=%fused_computation.1 | convolution fusion | flops 53747712 | bytes 1743552 | tf_op jit(solution)/shard_map/cxyk,jy->cxjk/dot_general | solution.py:138
  21.5 1.6 %convolution_bitcast_fusion.1 = f32[3,18,18,144]{3,1,2,0:T(8,128)S(1)} fusion(f32[18,24,1,1]{1,0,3,2:T(8,128)S(1)} %copy-done.4, f32[3,24,18,144]{3,2,1,0:T(8,128)S(1)} %convolution_bitcast_fusion), kind=kOutput, calls=%fused_computation.2 | convolution fusion | flops 40310784 | bytes 1308096 | tf_op jit(solution)/shard_map/cxjk,ix->cijk/dot_general | solution.py:144
  23.1 0.3 copy.30
  23.5 6.3 %reshape.6592 = f32[3,2,9,2,9,16,9]{6,5,4,3,2,1,0:T(8,128)} reshape(f32[3,18,18,144]{3,2,1,0:T(8,128)S(1)} %copy.30) | data formatting | bytes 1119744 | tf_op jit(solution)/shard_map/reshape | solution.py:161
  29.8 11.0 %copy.31 = f32[3,9,9,9,2,2,16]{6,5,4,0,3,2,1:T(2,128)} copy(f32[3,9,9,9,2,2,16]{3,6,2,5,1,4,0:T(8,128)} %bitcast.897) | data formatting | bytes 1119744 | tf_op jit(solution)/shard_map/transpose | solution.py:162
  40.8 5.8 %reshape.6593 = f32[3,9,9,9,64]{4,0,3,2,1:T(4,128)S(1)} reshape(f32[3,9,9,9,2,2,16]{6,5,4,0,3,2,1:T(2,128)} %copy.31) | data formatting | bytes 1119744 | tf_op jit(solution)/shard_map/reshape | solution.py:162
  46.7 0.8 fusion.125
  47.9 0.6 copy-done.5
  48.5 2.9 %fusion.158 = f32[6,24,24,32]{3,2,1,0:T(8,128)S(1)} fusion(f32[6,24,24,136]{3,2,1,0:T(8,128)S(1)} %multiply_dynamic-update-slice_fusion, f32[32,136,1,1]{1,0,3,2:T(8,128)S(1)} %copy-done.5), kind=kOutput, calls=%fused_computation.409 | convolution fusion | flops 180486144 | bytes 2339840 | tf_op jit(solution)/shard_map/cxyz,kz->cxyk/dot_general | solution.py:132
  51.4 1.0 convolution_bitcast_fusion.2
  52.5 0.3 convolution_bitcast_fusion.3
  52.8 0.2 copy.28
  52.9 2.0 %slice_reduce_fusion = (f32[2,2,16]{2,1,0:T(2,128)S(1)}, f32[2,2,16]{2,1,0:T(2,128)S(1)}, f32[2,2,16]{2,1,0:T(2,128)S(1)}, f32[2,2,16]{2,1,0:T(2,128)S(1)}, f32[...) fusion(f32[6,2,2,2,2,16,2]{0,6,5,4,3,2,1:T(2,128)S(1)} %bitcast.898), kind=kLoop, calls=%fused_computation.34 | loop fusion | bytes 6144 | tf_op jit(solution)/shard_map/slice | solution.py:97
  55.0 0.1 squeeze.35
  55.1 0.1 squeeze.34
  55.1 0.1 squeeze.33
  55.2 0.1 squeeze.32
  55.5 0.1 squeeze.29
  55.6 0.1 squeeze.27
  56.4 0.3 stack.8
  56.7 0.3 concatenate.21
  57.0 0.2 fusion.159
  57.3 40.3 %psum.7 = f32[102,102]{1,0:T(8,128)S(1)} all-reduce(f32[102,102]{1,0:T(8,128)S(1)} %fusion.159), channel_id=1, replica_groups=mesh['gx'=4,'gy'=4,'gz'=2] {'gx','gy','gz'}, use_global_device_ids=true, to_apply=%region_0.0 | all-reduce | flops 10404 | bytes 83232 | tf_op jit(solution)/shard_map/psum | solution.py:174
  97.6 1.7 %gather_fusion = f32[102]{0:T(128)S(1)} fusion(f32[102,102]{1,0:T(8,128)S(1)} %psum.7, s32[102]{0:T(128)S(1)} %or_bitcast_fusion), kind=kCustom, calls=%fused_computation | custom fusion | bytes 1632 | tf_op jit(solution)/shard_map/jit(diagonal)/cond/branch_0_fun/gather | solution.py:108
  99.3 0.1 fusion.5
  99.5 0.1 fusion.8
  99.6 8.8 %cholesky.16 = f32[96,96]{1,0:T(8,128)S(1)} custom-call(f32[96,96]{1,0:T(8,128)S(1)} %fusion.8), custom_call_target="Cholesky" | custom-call | tf_op jit(solution)/shard_map/jit(cholesky)/cholesky | solution.py:114
  108.4 0.6 compare_reduce_fusion
  109.1 0.7 fusion.3
  109.7 7.4 %custom-call.10 = f32[1,96,96]{1,2,0:T(8,128)S(1)} custom-call(f32[1,96,96]{2,1,0:T(8,128)S(1)} %fusion.3), custom_call_target="InvertDiagBlocksLowerTriangular" | custom-call | tf_op jit(solution)/shard_map/jit(_cho_solve)/triangular_solve | solution.py:115
  117.1 0.3 fusion.4
  117.4 0.2 convolution_divide_fusion
  117.6 0.8 fusion.1
  (62 shorter events, 1.6 us)
Async XLA Ops:
  1.7 16.9 %copy-start.8 = (f32[144,136,1,1]{0,1,3,2:T(8,128)S(1)}, f32[144,136,1,1]{0,1,3,2:T(8,128)}, u32[]{:S(2)}) copy-start(f32[144,136,1,1]{0,1,3,2:T(8,128)} %constant.98) | copy-start | bytes 235012
  1.7 7.3 %collective-permute-start = (bf16[3,4,16,128]{3,2,1,0:T(8,128)(2,1)S(1)}, bf16[3,4,16,128]{3,2,1,0:T(8,128)(2,1)S(1)}, u32[]{:S(2)}, u32[]{:S(2)}) collective-permute-start(bf16[3,4,16,128]{3,2,1,0:T(8,128)(2,1)S(1)} %get-tuple-element.102), channel_id=1, source_target_pairs={{0,8},{8,16},{16,24},{24,0},{1,9},{9,17},{17,25},{25,1},{2,10},{10... | collective-permute-start | bytes 147464 | tf_op jit(solution)/shard_map/ppermute | solution.py:18
  4.8 4.6 %collective-permute-start.1 = (bf16[3,4,16,128]{3,2,1,0:T(8,128)(2,1)S(1)}, bf16[3,4,16,128]{3,2,1,0:T(8,128)(2,1)S(1)}, u32[]{:S(2)}, u32[]{:S(2)}) collective-permute-start(bf16[3,4,16,128]{3,2,1,0:T(8,128)(2,1)S(1)} %get-tuple-element.103), channel_id=1, source_target_pairs={{8,0},{16,8},{24,16},{0,24},{9,1},{17,9},{25,17},{1,25},{10,2},{18... | collective-permute-start | bytes 147464 | tf_op jit(solution)/shard_map/ppermute | solution.py:21
  9.4 10.5 %copy-start.2 = (bf16[3,4,16,128]{3,2,1,0:T(8,128)(2,1)}, bf16[3,4,16,128]{3,2,1,0:T(8,128)(2,1)S(1)}, u32[]{:S(2)}) copy-start(bf16[3,4,16,128]{3,2,1,0:T(8,128)(2,1)S(1)} %collective-permute-done.1) | copy-start | bytes 147460
  9.5 5.3 %collective-permute-start.2 = (bf16[3,24,4,128]{3,2,1,0:T(4,128)(2,1)S(1)}, bf16[3,24,4,128]{3,2,1,0:T(4,128)(2,1)S(1)}, u32[]{:S(2)}, u32[]{:S(2)}) collective-permute-start(bf16[3,24,4,128]{3,2,1,0:T(4,128)(2,1)S(1)} %get-tuple-element.100), channel_id=1, source_target_pairs={{0,2},{2,4},{4,6},{6,0},{1,3},{3,5},{5,7},{7,1},{8,10},{10,12},{12... | collective-permute-start | bytes 221192 | tf_op jit(solution)/shard_map/ppermute | solution.py:18
  11.0 4.6 %collective-permute-start.3 = (bf16[3,24,4,128]{3,2,1,0:T(4,128)(2,1)S(1)}, bf16[3,24,4,128]{3,2,1,0:T(4,128)(2,1)S(1)}, u32[]{:S(2)}, u32[]{:S(2)}) collective-permute-start(bf16[3,24,4,128]{3,2,1,0:T(4,128)(2,1)S(1)} %get-tuple-element.101), channel_id=1, source_target_pairs={{2,0},{4,2},{6,4},{0,6},{3,1},{5,3},{7,5},{1,7},{10,8},{12,10},{14... | collective-permute-start | bytes 221192 | tf_op jit(solution)/shard_map/ppermute | solution.py:21
  16.1 1.9 %collective-permute-start.4 = (bf16[3,24,24,4]{3,2,1,0:T(8,128)(2,1)S(1)}, bf16[3,24,24,4]{3,2,1,0:T(8,128)(2,1)S(1)}, u32[]{:S(2)}, u32[]{:S(2)}) collective-permute-start(bf16[3,24,24,4]{3,2,1,0:T(8,128)(2,1)S(1)} %get-tuple-element.98), channel_id=1, source_target_pairs={{0,1},{1,0},{2,3},{3,2},{4,5},{5,4},{6,7},{7,6},{8,9},{9,8},{10,11... | collective-permute-start | bytes 41480 | tf_op jit(solution)/shard_map/ppermute | solution.py:18
  16.2 2.4 %collective-permute-start.5 = (bf16[3,24,24,4]{3,2,1,0:T(8,128)(2,1)S(1)}, bf16[3,24,24,4]{3,2,1,0:T(8,128)(2,1)S(1)}, u32[]{:S(2)}, u32[]{:S(2)}) collective-permute-start(bf16[3,24,24,4]{3,2,1,0:T(8,128)(2,1)S(1)} %get-tuple-element.99), channel_id=1, source_target_pairs={{1,0},{0,1},{3,2},{2,3},{5,4},{4,5},{7,6},{6,7},{9,8},{8,9},{11,10... | collective-permute-start | bytes 41480 | tf_op jit(solution)/shard_map/ppermute | solution.py:21
  16.7 3.3 %copy-start.4 = (f32[18,24,1,1]{1,0,3,2:T(8,128)S(1)}, f32[18,24,1,1]{1,0,3,2:T(8,128)}, u32[]{:S(2)}) copy-start(f32[18,24,1,1]{1,0,3,2:T(8,128)} %constant.99) | copy-start | bytes 5188
  18.6 1.3 %copy-start = (bf16[3,24,24,4]{3,2,1,0:T(8,128)(2,1)}, bf16[3,24,24,4]{3,2,1,0:T(8,128)(2,1)S(1)}, u32[]{:S(2)}) copy-start(bf16[3,24,24,4]{3,2,1,0:T(8,128)(2,1)S(1)} %collective-permute-done.5) | copy-start | bytes 41476
  40.8 5.9 %copy-start.1 = (bf16[3,24,24,4]{3,2,1,0:T(8,128)(2,1)S(1)}, bf16[3,24,24,4]{3,2,1,0:T(8,128)(2,1)}, u32[]{:S(2)}) copy-start(bf16[3,24,24,4]{3,2,1,0:T(8,128)(2,1)} %copy-done) | copy-start | bytes 41476
  40.8 5.9 %copy-start.3 = (bf16[3,4,16,128]{3,2,1,0:T(8,128)(2,1)S(1)}, bf16[3,4,16,128]{3,2,1,0:T(8,128)(2,1)}, u32[]{:S(2)}) copy-start(bf16[3,4,16,128]{3,2,1,0:T(8,128)(2,1)} %copy-done.2) | copy-start | bytes 147460
  47.7 0.8 copy-start.5
  48.5 2.9 %copy-start.6 = (f32[4,24,1,1]{1,0,3,2:T(4,128)S(1)}, f32[4,24,1,1]{1,0,3,2:T(4,128)}, u32[]{:S(2)}) copy-start(f32[4,24,1,1]{1,0,3,2:T(4,128)} %constant.97) | copy-start | bytes 1156
  117.6 0.8 copy-start.7
where the time goes:
time: 119 us; the launch traced here: 118 us
  blocking collectives  40.3 us (34%)
  local copies, waits for them, and re-layouts  29.8 us (25%)
  other arithmetic  20.6 us (17%)
  matrix products  10.3 us (9%)
  starting transfers between devices  8.74 us (7%)
  waiting for transfers between devices  7.6 us (6%)
    psum x1, blocking collectives, shards(): gram_matrix = lax.psum(local_gram, ('gx', 'gy', 'gz'))  40.3 us
    transpose x1, local copies, waits for them, and re-layouts, shards(): jnp.transpose(box_means, (0, 2, 4, 6, 1, 3, 5)).reshape(3, 9, 9, 9, samples)  11 us
    another operation x3, other arithmetic, solve_fit(): factor = jnp.linalg.cholesky(normal)  9.45 us
    another operation x2, other arithmetic, solve_fit(): solved = jax.scipy.linalg.cho_solve((factor, True), target_side)  8.01 us
    reshape x1, local copies, waits for them, and re-layouts, shards(): box_means = box_means.reshape(3, count_x, 9, count_y, 9, count_z, 9)  6.35 us
    reshape x1, local copies, waits for them, and re-layouts, shards(): jnp.transpose(box_means, (0, 2, 4, 6, 1, 3, 5)).reshape(3, 9, 9, 9, samples)  5.76 us
    ppermute x3, waiting for transfers between devices, extended(): lax.ppermute(lax.slice_in_dim(block, block.shape[dim] - width, None, axis...  5.7 us
    ppermute x3, starting transfers between devices, extended(): lax.ppermute(lax.slice_in_dim(block, block.shape[dim] - width, None, axis...  4.72 us
  transfers between devices with their start and end apart: 6, of which 6 were waited for; matrix products, arithmetic and copies ran while one was open for 0% of the time, Pallas kernels for 0%

commit v1 on v0

--- a/solution.py
+++ b/solution.py
@@ -171,7 +171,7 @@
     features, targets = build_rows(box_means, pair_means)
     stacked = jnp.concatenate([features, targets], axis=0)
     local_gram = jnp.dot(stacked, stacked.T, precision=PRECISE, preferred_element_type=jnp.float32)
-    gram_matrix = lax.psum(local_gram, ("gx", "gy", "gz"))
+    gram_matrix = jnp.sum(jax.lax.all_gather(local_gram, ("gx", "gy", "gz")), axis=0)
     sample_total = float(samples * lax.axis_size("gx") * lax.axis_size("gy") * lax.axis_size("gz"))
     coefficients, target_scale = solve_fit(gram_matrix, sample_total)
     predicted = jnp.dot(

time: 119 us -> 150 us (1.26)
  waiting for transfers between devices: 7.6 us -> 63.5 us
  blocking collectives: 40.3 us -> 0 us
  between operations: 1.07 us -> 14.4 us
  other arithmetic: 20.6 us -> 22.2 us
    all_gather x0 -> x1, waiting for transfers between devices: none -> 55.9 us  [shards(): jax.lax.all_gather(local_gram, ('gx', 'gy', 'gz'))]
    psum x1 -> x0, blocking collectives: 40.3 us -> none  [shards(): gram_matrix = lax.psum(local_gram, ('gx', 'gy', 'gz'))]
    reduce_sum x0 -> x1, other arithmetic: none -> 1.59 us  [shards(): jnp.sum(jax.lax.all_gather(local_gram, ('gx', 'gy', 'gz')), axis=0)]
  transfers between devices with their start and end apart: 6 -> 7, of which waited for: 6 -> 7; matrix products, arithmetic and copies ran while one was open for 0% -> 0% of each run, Pallas kernels for 0% -> 0%
where the time goes in v1:
time: 150 us
  waiting for transfers between devices  63.5 us (42%)
  local copies, waits for them, and re-layouts  30 us (20%)
  other arithmetic  22.2 us (15%)
  between operations  14.4 us (10%)
  matrix products  10.9 us (7%)
  starting transfers between devices  8.77 us (6%)
    all_gather x1, waiting for transfers between devices, shards(): jax.lax.all_gather(local_gram, ('gx', 'gy', 'gz'))  55.9 us
    transpose x1, local copies, waits for them, and re-layouts, shards(): jnp.transpose(box_means, (0, 2, 4, 6, 1, 3, 5)).reshape(3, 9, 9, 9, samples)  10.9 us
    another operation x3, other arithmetic, solve_fit(): factor = jnp.linalg.cholesky(normal)  9.45 us
    another operation x2, other arithmetic, solve_fit(): solved = jax.scipy.linalg.cho_solve((factor, True), target_side)  8.01 us
    reshape x1, local copies, waits for them, and re-layouts, shards(): box_means = box_means.reshape(3, count_x, 9, count_y, 9, count_z, 9)  6.35 us
    ppermute x3, waiting for transfers between devices, extended(): lax.ppermute(lax.slice_in_dim(block, block.shape[dim] - width, None, axis...  5.71 us
    reshape x1, local copies, waits for them, and re-layouts, shards(): jnp.transpose(box_means, (0, 2, 4, 6, 1, 3, 5)).reshape(3, 9, 9, 9, samples)  5.7 us
    ppermute x3, starting transfers between devices, extended(): lax.ppermute(lax.slice_in_dim(block, block.shape[dim] - width, None, axis...  4.72 us
  transfers between devices with their start and end apart: 7, of which 7 were waited for; matrix products, arithmetic and copies ran while one was open for 0% of the time, Pallas kernels for 0%

profile of v1, /device:TPU:0, one launch (start us, length us, event | category | flops | bytes accessed | tf_op | source)
XLA Modules:
  0.0 149.7 jit_solution(12968100625260086564)
XLA Ops:
  7.2 1.0 convert_element_type.7
  8.3 3.1 %collective-permute-start = (bf16[3,4,16,128]{3,2,1,0:T(8,128)(2,1)S(1)}, bf16[3,4,16,128]{3,2,1,0:T(8,128)(2,1)S(1)}, u32[]{:S(2)}, u32[]{:S(2)}) collective-permute-start(bf16[3,4,16,128]{3,2,1,0:T(8,128)(2,1)S(1)} %get-tuple-element.102), channel_id=1, source_target_pairs={{0,8},{8,16},{16,24},{24,0},{1,9},{9,17},{17,25},{25,1},{2,10},{10... | collective-permute-start | bytes 147464 | tf_op jit(solution)/shard_map/ppermute | solution.py:18
  11.4 2.1 %collective-permute-start.1 = (bf16[3,4,16,128]{3,2,1,0:T(8,128)(2,1)S(1)}, bf16[3,4,16,128]{3,2,1,0:T(8,128)(2,1)S(1)}, u32[]{:S(2)}, u32[]{:S(2)}) collective-permute-start(bf16[3,4,16,128]{3,2,1,0:T(8,128)(2,1)S(1)} %get-tuple-element.103), channel_id=1, source_target_pairs={{8,0},{16,8},{24,16},{0,24},{9,1},{17,9},{25,17},{1,25},{10,2},{18... | collective-permute-start | bytes 147464 | tf_op jit(solution)/shard_map/ppermute | solution.py:21
  13.5 2.1 %collective-permute-done = bf16[3,4,16,128]{3,2,1,0:T(8,128)(2,1)S(1)} collective-permute-done((bf16[3,4,16,128]{3,2,1,0:T(8,128)(2,1)S(1)}, bf16[3,4,16,128]{3,2,1,0:T(8,128)(2,1)S(1)}, u32[]{:S(2)}, u32[]{:S(2)}) %collective-permute-start) | collective-permute-done | bytes 49184 | tf_op jit(solution)/shard_map/ppermute | solution.py:18
  15.6 0.4 collective-permute-done.1
  16.1 1.5 %collective-permute-start.2 = (bf16[3,24,4,128]{3,2,1,0:T(4,128)(2,1)S(1)}, bf16[3,24,4,128]{3,2,1,0:T(4,128)(2,1)S(1)}, u32[]{:S(2)}, u32[]{:S(2)}) collective-permute-start(bf16[3,24,4,128]{3,2,1,0:T(4,128)(2,1)S(1)} %get-tuple-element.100), channel_id=1, source_target_pairs={{0,2},{2,4},{4,6},{6,0},{1,3},{3,5},{5,7},{7,1},{8,10},{10,12},{12... | collective-permute-start | bytes 221192 | tf_op jit(solution)/shard_map/ppermute | solution.py:18
  17.6 1.4 collective-permute-start.3
  19.0 2.3 %collective-permute-done.2 = bf16[3,24,4,128]{3,2,1,0:T(4,128)(2,1)S(1)} collective-permute-done((bf16[3,24,4,128]{3,2,1,0:T(4,128)(2,1)S(1)}, bf16[3,24,4,128]{3,2,1,0:T(4,128)(2,1)S(1)}, u32[]{:S(2)}, u32[]{:S(2)}) %collective-permute-start.2) | collective-permute-done | bytes 73760 | tf_op jit(solution)/shard_map/ppermute | solution.py:18
  21.4 0.8 collective-permute-done.3
  22.2 0.2 pad_maximum_fusion.1
  22.5 0.2 fusion.156
  22.7 0.5 collective-permute-start.5
  23.2 1.3 collective-permute-done.4
  24.5 0.6 collective-permute-done.5
  25.1 1.3 fusion.124
  26.5 1.6 %convolution_bitcast_fusion = f32[3,24,18,144]{3,2,1,0:T(8,128)S(1)} fusion(f32[3,24,24,144]{3,2,1,0:T(8,128)S(1)} %fusion.124, f32[18,24,1,1]{1,0,3,2:T(8,128)S(1)} %copy-done), kind=kOutput, calls=%fused_computation.1 | convolution fusion | flops 53747712 | bytes 1743552 | tf_op jit(solution)/shard_map/cxyk,jy->cxjk/dot_general | solution.py:138
  28.1 1.6 %convolution_bitcast_fusion.1 = f32[3,18,18,144]{3,1,2,0:T(8,128)S(1)} fusion(f32[18,24,1,1]{1,0,3,2:T(8,128)S(1)} %copy-done, f32[3,24,18,144]{3,2,1,0:T(8,128)S(1)} %convolution_bitcast_fusion), kind=kOutput, calls=%fused_computation.2 | convolution fusion | flops 40310784 | bytes 1308096 | tf_op jit(solution)/shard_map/cxjk,ix->cijk/dot_general | solution.py:144
  29.7 0.3 copy.36
  30.0 6.3 %reshape.6592 = f32[3,2,9,2,9,16,9]{6,5,4,3,2,1,0:T(8,128)} reshape(f32[3,18,18,144]{3,2,1,0:T(8,128)S(1)} %copy.36) | data formatting | bytes 1119744 | tf_op jit(solution)/shard_map/reshape | solution.py:161
  36.4 10.9 %copy.37 = f32[3,9,9,9,2,2,16]{6,5,4,0,3,2,1:T(2,128)} copy(f32[3,9,9,9,2,2,16]{3,6,2,5,1,4,0:T(8,128)} %bitcast.899) | data formatting | bytes 1119744 | tf_op jit(solution)/shard_map/transpose | solution.py:162
  47.3 5.7 %reshape.6593 = f32[3,9,9,9,64]{4,0,3,2,1:T(4,128)S(1)} reshape(f32[3,9,9,9,2,2,16]{6,5,4,0,3,2,1:T(2,128)} %copy.37) | data formatting | bytes 1119744 | tf_op jit(solution)/shard_map/reshape | solution.py:162
  53.1 0.8 fusion.125
  54.4 0.6 copy-done.1
  54.9 2.9 %fusion.158 = f32[6,24,24,32]{3,2,1,0:T(8,128)S(1)} fusion(f32[6,24,24,136]{3,2,1,0:T(8,128)S(1)} %multiply_dynamic-update-slice_fusion, f32[32,136,1,1]{1,0,3,2:T(8,128)S(1)} %copy-done.1), kind=kOutput, calls=%fused_computation.410 | convolution fusion | flops 180486144 | bytes 2339840 | tf_op jit(solution)/shard_map/cxyz,kz->cxyk/dot_general | solution.py:132
  57.9 1.0 convolution_bitcast_fusion.2
  58.9 0.3 convolution_bitcast_fusion.4
  59.2 0.2 copy.34
  59.4 2.0 %slice_reduce_fusion = (f32[2,2,16]{2,1,0:T(2,128)S(1)}, f32[2,2,16]{2,1,0:T(2,128)S(1)}, f32[2,2,16]{2,1,0:T(2,128)S(1)}, f32[2,2,16]{2,1,0:T(2,128)S(1)}, f32[...) fusion(f32[6,2,2,2,2,16,2]{0,6,5,4,3,2,1:T(2,128)S(1)} %bitcast.900), kind=kLoop, calls=%fused_computation.35 | loop fusion | bytes 6144 | tf_op jit(solution)/shard_map/slice | solution.py:97
  61.4 0.1 squeeze.35
  61.5 0.1 squeeze.34
  61.6 0.1 squeeze.33
  61.8 0.1 squeeze.30
  62.3 0.1 squeeze.25
  62.9 0.3 concatenate.21
  63.2 0.9 convolution_bitcast_fusion.3
  64.1 0.3 stack.8
  64.4 55.9 %all-gather.4.cloned.1.call-done = f32[32,102,102]{2,1,0:T(8,128)} async-done(((f32[1,102,102]{2,1,0:T(8,128)}), f32[32,102,102]{2,1,0:T(8,128)}) %all-gather.4.cloned.1.call-update) | async-done | bytes 1331728 | tf_op jit(solution)/shard_map/all_gather | solution.py:174
  120.2 1.6 %reduce_sum.9 = f32[102,102]{1,0:T(8,128)S(1)} reduce(f32[32,102,102]{2,1,0:T(8,128)} %all-gather.4.cloned.1.call-done, f32[]{:T(128)} %constant.73.clone.1), dimensions={0}, to_apply=%region_0.0 | reduce | flops 322524 | bytes 1373332 | tf_op jit(solution)/shard_map/reduce_sum | solution.py:174
  121.8 1.9 %gather_fusion = f32[102]{0:T(128)S(1)} fusion(f32[102,102]{1,0:T(8,128)S(1)} %reduce_sum.9, s32[102]{0:T(128)S(1)} %or_bitcast_fusion), kind=kCustom, calls=%fused_computation | custom fusion | bytes 1632 | tf_op jit(solution)/shard_map/jit(diagonal)/cond/branch_0_fun/gather | solution.py:108
  123.8 0.1 fusion.5
  124.0 0.1 fusion.8
  124.1 8.8 %cholesky.16 = f32[96,96]{1,0:T(8,128)S(1)} custom-call(f32[96,96]{1,0:T(8,128)S(1)} %fusion.8), custom_call_target="Cholesky" | custom-call | tf_op jit(solution)/shard_map/jit(cholesky)/cholesky | solution.py:114
  132.9 0.6 compare_reduce_fusion
  133.6 0.7 fusion.3
  134.2 7.4 %custom-call.10 = f32[1,96,96]{1,2,0:T(8,128)S(1)} custom-call(f32[1,96,96]{2,1,0:T(8,128)S(1)} %fusion.3), custom_call_target="InvertDiagBlocksLowerTriangular" | custom-call | tf_op jit(solution)/shard_map/jit(_cho_solve)/triangular_solve | solution.py:115
  141.6 0.3 fusion.4
  141.9 0.2 convolution_divide_fusion
  142.1 0.8 fusion.1
  (57 shorter events, 1.8 us)
Async XLA Ops:
  7.2 113.1 %all-gather.4.cloned.1.call-start = ((), (), s32[]{:S(2)}) async-start(), calls=%async_computation | async-start | bytes 1757184 | tf_op jit(solution)/shard_map/all_gather | solution.py:174
  8.2 16.9 %copy-start.4 = (f32[144,136,1,1]{0,1,3,2:T(8,128)S(1)}, f32[144,136,1,1]{0,1,3,2:T(8,128)}, u32[]{:S(2)}) copy-start(f32[144,136,1,1]{0,1,3,2:T(8,128)} %constant.99) | copy-start | bytes 235012
  8.3 7.3 %collective-permute-start = (bf16[3,4,16,128]{3,2,1,0:T(8,128)(2,1)S(1)}, bf16[3,4,16,128]{3,2,1,0:T(8,128)(2,1)S(1)}, u32[]{:S(2)}, u32[]{:S(2)}) collective-permute-start(bf16[3,4,16,128]{3,2,1,0:T(8,128)(2,1)S(1)} %get-tuple-element.102), channel_id=1, source_target_pairs={{0,8},{8,16},{16,24},{24,0},{1,9},{9,17},{17,25},{25,1},{2,10},{10... | collective-permute-start | bytes 147464 | tf_op jit(solution)/shard_map/ppermute | solution.py:18
  11.4 4.6 %collective-permute-start.1 = (bf16[3,4,16,128]{3,2,1,0:T(8,128)(2,1)S(1)}, bf16[3,4,16,128]{3,2,1,0:T(8,128)(2,1)S(1)}, u32[]{:S(2)}, u32[]{:S(2)}) collective-permute-start(bf16[3,4,16,128]{3,2,1,0:T(8,128)(2,1)S(1)} %get-tuple-element.103), channel_id=1, source_target_pairs={{8,0},{16,8},{24,16},{0,24},{9,1},{17,9},{25,17},{1,25},{10,2},{18... | collective-permute-start | bytes 147464 | tf_op jit(solution)/shard_map/ppermute | solution.py:21
  16.1 5.3 %collective-permute-start.2 = (bf16[3,24,4,128]{3,2,1,0:T(4,128)(2,1)S(1)}, bf16[3,24,4,128]{3,2,1,0:T(4,128)(2,1)S(1)}, u32[]{:S(2)}, u32[]{:S(2)}) collective-permute-start(bf16[3,24,4,128]{3,2,1,0:T(4,128)(2,1)S(1)} %get-tuple-element.100), channel_id=1, source_target_pairs={{0,2},{2,4},{4,6},{6,0},{1,3},{3,5},{5,7},{7,1},{8,10},{10,12},{12... | collective-permute-start | bytes 221192 | tf_op jit(solution)/shard_map/ppermute | solution.py:18
  17.6 4.6 %collective-permute-start.3 = (bf16[3,24,4,128]{3,2,1,0:T(4,128)(2,1)S(1)}, bf16[3,24,4,128]{3,2,1,0:T(4,128)(2,1)S(1)}, u32[]{:S(2)}, u32[]{:S(2)}) collective-permute-start(bf16[3,24,4,128]{3,2,1,0:T(4,128)(2,1)S(1)} %get-tuple-element.101), channel_id=1, source_target_pairs={{2,0},{4,2},{6,4},{0,6},{3,1},{5,3},{7,5},{1,7},{10,8},{12,10},{14... | collective-permute-start | bytes 221192 | tf_op jit(solution)/shard_map/ppermute | solution.py:21
  22.7 1.9 %collective-permute-start.4 = (bf16[3,24,24,4]{3,2,1,0:T(8,128)(2,1)S(1)}, bf16[3,24,24,4]{3,2,1,0:T(8,128)(2,1)S(1)}, u32[]{:S(2)}, u32[]{:S(2)}) collective-permute-start(bf16[3,24,24,4]{3,2,1,0:T(8,128)(2,1)S(1)} %get-tuple-element.98), channel_id=1, source_target_pairs={{0,1},{1,0},{2,3},{3,2},{4,5},{5,4},{6,7},{7,6},{8,9},{9,8},{10,11... | collective-permute-start | bytes 41480 | tf_op jit(solution)/shard_map/ppermute | solution.py:18
  22.7 3.7 %copy-start = (f32[18,24,1,1]{1,0,3,2:T(8,128)S(1)}, f32[18,24,1,1]{1,0,3,2:T(8,128)}, u32[]{:S(2)}) copy-start(f32[18,24,1,1]{1,0,3,2:T(8,128)} %constant.100) | copy-start | bytes 5188
  22.7 2.4 %collective-permute-start.5 = (bf16[3,24,24,4]{3,2,1,0:T(8,128)(2,1)S(1)}, bf16[3,24,24,4]{3,2,1,0:T(8,128)(2,1)S(1)}, u32[]{:S(2)}, u32[]{:S(2)}) collective-permute-start(bf16[3,24,24,4]{3,2,1,0:T(8,128)(2,1)S(1)} %get-tuple-element.99), channel_id=1, source_target_pairs={{1,0},{0,1},{3,2},{2,3},{5,4},{4,5},{7,6},{6,7},{9,8},{8,9},{11,10... | collective-permute-start | bytes 41480 | tf_op jit(solution)/shard_map/ppermute | solution.py:21
  54.2 0.8 copy-start.1
  54.9 2.9 %copy-start.2 = (f32[4,24,1,1]{1,0,3,2:T(4,128)S(1)}, f32[4,24,1,1]{1,0,3,2:T(4,128)}, u32[]{:S(2)}) copy-start(f32[4,24,1,1]{1,0,3,2:T(4,128)} %constant.98) | copy-start | bytes 1156
  142.1 0.8 copy-start.3
Sparse Core Ops, SparseCore 0:
  64.2 56.0 all-gather.3
